TPU v7x, 32 devices: a whole 2x2x4 slice. The times are simulated.
32 devices in a mesh: tm: 4 (over z), tmpl: 8 (over y, x, core).
Axes of the slice: x: 2, y: 2, z: 4, core: 2. Of those that a mesh axis runs over, the one named last changes fastest.
Arguments:
- strain: float32 [8, 131072], P('tmpl', 'tm'), may hold values from -6 to 6
- psd_bins: int32 [4, 65536], P(None, 'tmpl'), may hold values from 0 to 8191, as said below
- psd_values: float32 [4, 8192], P('tm'), may hold values from 0.25 to 4
- chirp_slope: int32 [16], P('tmpl'), may hold values from 0 to 1023
- chirp_curve: int32 [16], P('tmpl'), may hold values from 1 to 63
Outputs:
- snr: float32 [16, 1048576], P('tmpl', 'tm')
Inputs may be any that keep to these rules, and one draw needn't show every extreme that they name: psd_bins[r, c] names the row of psd_values that serves frequency bin r * 65536 + c.
All inputs are finite; a program needn't handle non-finite values.
Results may differ from a plain program's by a relative error of at most 0.0003.
Values sent between devices are 32-bit elements; how exact they have to be, the bound alone decides.
A program may use at most 128 MiB of HBM per device.

v0:
```python
import math
import jax
import jax.numpy as jnp
from jax import lax
from jax.sharding import PartitionSpec as P

OR = 32768
HIGHEST = lax.Precision.HIGHEST
TWO_PI = 2.0 * math.pi


def shifted(block, axis, distance):
    devices = range(lax.axis_size(axis))
    route = [(i - distance, i) for i in devices if i - distance in devices]
    return lax.ppermute(block, axis, route)


def split_sizes(length):
    count = 0
    while length > 512:
        length = length // 128
        count = count + 1
    return [length] + [128] * count


def angle_table(rows_count, cols_count, modulus, direction):
    product = (
        jnp.arange(rows_count, dtype=jnp.int32)[:, None]
        * jnp.arange(cols_count, dtype=jnp.int32)[None, :]
    )
    angles = (product % modulus).astype(jnp.float32) * (direction * TWO_PI / modulus)
    return (jnp.cos(angles), jnp.sin(angles))


def complex_left(cos_part, sin_part, real_part, imag_part):
    new_re = jnp.einsum("qp,...pk->...qk", cos_part, real_part, precision=HIGHEST) - jnp.einsum(
        "qp,...pk->...qk", sin_part, imag_part, precision=HIGHEST
    )
    new_im = jnp.einsum("qp,...pk->...qk", sin_part, real_part, precision=HIGHEST) + jnp.einsum(
        "qp,...pk->...qk", cos_part, imag_part, precision=HIGHEST
    )
    return (new_re, new_im)


def apply_sizes(real_part, imag_part, sizes, direction):
    length = real_part.shape[-1]
    if len(sizes) == 1:
        cos_part, sin_part = angle_table(length, length, length, direction)
        new_re = jnp.matmul(real_part, cos_part, precision=HIGHEST) - jnp.matmul(
            imag_part, sin_part, precision=HIGHEST
        )
        new_im = jnp.matmul(real_part, sin_part, precision=HIGHEST) + jnp.matmul(
            imag_part, cos_part, precision=HIGHEST
        )
        return (new_re, new_im)
    outer_size = sizes[0]
    inner_size = length // outer_size
    leading = real_part.shape[:-1]
    real_part = real_part.reshape(leading + (outer_size, inner_size))
    imag_part = imag_part.reshape(leading + (outer_size, inner_size))
    mat_cos, mat_sin = angle_table(outer_size, outer_size, outer_size, direction)
    real_part, imag_part = complex_left(mat_cos, mat_sin, real_part, imag_part)
    cos_part, sin_part = angle_table(outer_size, inner_size, length, direction)
    real_part, imag_part = (
        real_part * cos_part - imag_part * sin_part,
        real_part * sin_part + imag_part * cos_part,
    )
    return apply_sizes(real_part, imag_part, sizes[1:], direction)


def transform(real_part, imag_part, direction):
    length = real_part.shape[-1]
    leading = real_part.shape[:-1]
    sizes = split_sizes(length)
    new_re, new_im = apply_sizes(real_part, imag_part, sizes, direction)
    lead_count = len(leading)
    last_axis = new_re.ndim - 1
    order = tuple(range(lead_count)) + tuple(range(last_axis, lead_count - 1, -1))
    new_re = jnp.transpose(new_re, order)
    new_im = jnp.transpose(new_im, order)
    return (new_re.reshape(leading + (length,)), new_im.reshape(leading + (length,)))


def chirp_phase(frequency, slope, curve, modulus):
    high_part = frequency // 1024
    low_part = frequency % 1024
    square = 2 * high_part * low_part % (modulus // 1024) * 1024 + low_part * low_part
    square = square % modulus
    return (slope * frequency + curve * square) % modulus


def amplitude_of(frequency, k_low, k_cut):
    ratio = frequency.astype(jnp.float32) / k_low
    inside = (frequency >= k_low) & (frequency < k_cut)
    return jnp.where(inside, jnp.power(jnp.maximum(ratio, 1.0), -7.0 / 6.0), 0.0)


def template_parts(frequency, chirp_slope, chirp_curve, modulus, k_low, k_cut):
    phase = chirp_phase(frequency[None, :], chirp_slope[:, None], chirp_curve[:, None], modulus)
    angles = phase.astype(jnp.float32) * (TWO_PI / modulus)
    amplitude = amplitude_of(frequency, k_low, k_cut)
    return (amplitude * jnp.cos(angles), -amplitude * jnp.sin(angles))


def local(strain, psd_bins, psd_values, chirp_slope, chirp_curve):
    groups = lax.axis_size("tmpl")
    member = lax.axis_index("tmpl")
    own_part = strain[0]
    edge_tail = shifted(own_part, "tm", 1)
    local_seq = jnp.concatenate([edge_tail, own_part])
    sub_len = local_seq.shape[0]
    total_len = sub_len * groups
    block_len = sub_len // groups
    norm_scale = 1.0 / math.sqrt(total_len)
    k_low = total_len // 200
    k_cut = 3 * total_len // 8
    band_rows = 3 * groups // 8
    inv_psd = 1.0 / jnp.take(psd_values[0], psd_bins[:band_rows])
    local_re, local_im = transform(local_seq, jnp.zeros_like(local_seq), -1.0)
    index_k = jnp.arange(sub_len, dtype=jnp.int32)
    angles = (member * index_k % total_len).astype(jnp.float32) * (-TWO_PI / total_len)
    twist_cos = jnp.cos(angles)
    twist_sin = jnp.sin(angles)
    part_re = local_re * twist_cos - local_im * twist_sin
    part_im = local_re * twist_sin + local_im * twist_cos
    cross_cos, cross_sin = angle_table(band_rows, groups, groups, -1.0)
    piece_re = lax.all_to_all(
        part_re.reshape(groups, 1, block_len), "tmpl", split_axis=0, concat_axis=1, tiled=True
    )
    piece_im = lax.all_to_all(
        part_im.reshape(groups, 1, block_len), "tmpl", split_axis=0, concat_axis=1, tiled=True
    )
    spec_re, spec_im = complex_left(cross_cos, cross_sin, piece_re[0], piece_im[0])
    white_re = spec_re * inv_psd * norm_scale
    white_im = spec_im * inv_psd * norm_scale
    white_re, white_im, inv_whole = (
        lax.all_gather(white_re, "tmpl", axis=1, tiled=True),
        lax.all_gather(white_im, "tmpl", axis=1, tiled=True),
        lax.all_gather(inv_psd, "tmpl", axis=1, tiled=True),
    )
    band_len = band_rows * sub_len
    white_re = white_re.reshape(band_len)
    white_im = white_im.reshape(band_len)
    frequency = jnp.arange(band_len, dtype=jnp.int32)
    tmpl_re, tmpl_im = template_parts(frequency, chirp_slope, chirp_curve, total_len, k_low, k_cut)
    inv_whole = inv_whole.reshape(band_len)
    sigma_sq = jnp.sum((tmpl_re * tmpl_re + tmpl_im * tmpl_im) * inv_whole, axis=-1)
    coef_re = white_re * tmpl_re + white_im * tmpl_im
    coef_im = white_im * tmpl_re - white_re * tmpl_im
    widths = ((0, 0), (0, total_len - band_len))
    series_re, series_im = transform(jnp.pad(coef_re, widths), jnp.pad(coef_im, widths), 1.0)
    magnitude = (
        jnp.sqrt(series_re * series_re + series_im * series_im) / jnp.sqrt(sigma_sq)[..., None]
    )
    return magnitude[:, OR * groups :]


def solution(mesh):
    placed = (P("tmpl", "tm"), P(None, "tmpl"), P("tm", None), P("tmpl"), P("tmpl"))
    return jax.shard_map(
        local, mesh=mesh, in_specs=placed, out_specs=P("tmpl", "tm"), check_vma=False
    )
```

profile of v0, /device:TPU:0, one launch (start us, length us, event | category | flops | bytes accessed | tf_op | source)
XLA Modules:
  0.0 431.6 jit_solution(9449449563915326860)
XLA Ops:
  0.0 5.1 %collective-permute-start = (f32[32768]{0:T(1024)}, f32[32768]{0:T(1024)S(1)}, u32[]{:S(2)}, u32[]{:S(2)}) collective-permute-start(f32[32768]{0:T(1024)} %bitcast.131), channel_id=1, source_target_pairs={{0,8},{8,16},{16,24},{1,9},{9,17},{17,25},{2,10},{10,18},{18,26},{... | collective-permute-start | bytes 393224 | tf_op jit(solution)/shard_map/ppermute | solution.py:15
  5.1 5.9 %fusion.81 = f32[512,128]{1,0:T(8,128)} fusion(), kind=kOutput, calls=%fused_computation.114 | convolution fusion | flops 406323200 | bytes 262144 | tf_op jit(solution)/shard_map/qp,...pk->...qk/dot_general | solution.py:36
  11.0 1.7 add_select_fusion.2
  12.6 1.7 fusion.71
  14.3 9.1 %fusion.55 = (f32[32,16384]{1,0:T(8,128)S(1)}, f32[32,16384]{1,0:T(8,128)}) fusion(), kind=kLoop, calls=%fused_computation.91 | loop fusion | flops 7340032 | bytes 4194304 | tf_op jit(solution)/shard_map/sin | solution.py:32
  23.4 0.1 reshape.354
  23.6 135.5 %gather_fusion = f32[24576]{0:T(1024)S(1)} fusion(f32[8192]{0:T(1024)S(1)} %bitcast.120, s32[24576]{0:T(1024)S(1)} %broadcast_clamp_fusion), kind=kCustom, calls=%fused_computation | custom fusion | bytes 294912 | tf_op jit(solution)/shard_map/jit(_take)/gather | solution.py:118
  159.1 0.0 copy-start.7
  159.2 0.1 select_divide_fusion
  159.2 0.3 fusion.154
  159.5 0.1 copy.46
  159.6 5.5 %fusion.77 = f32[512,128]{1,0:T(8,128)S(1)} fusion(), kind=kOutput, calls=%fused_computation.113 | convolution fusion | flops 406323200 | bytes 262144 | tf_op jit(solution)/shard_map/qp,...pk->...qk/dot_general | solution.py:39
  165.1 0.0 collective-permute-done
  165.1 5.7 %convolution_subtract_fusion.3 = f32[512,128]{1,0:T(8,128)S(1)} fusion(f32[512,128]{1,0:T(8,128)} %fusion.81, f32[256,128]{1,0:T(8,128)S(1)} %bitcast.132, f32[256,128]{1,0:T(8,128)S(1)} %bitcast.134), kind=kOutput, calls=%fused_computation.87 | convolution fusion | flops 406454272 | bytes 786432 | tf_op jit(solution)/shard_map/qp,...pk->...qk/dot_general | solution.py:36
  170.8 4.8 %convolution_add_fusion.3 = f32[512,128]{1,0:T(8,128)S(1)} fusion(f32[512,128]{1,0:T(8,128)S(1)} %fusion.77, f32[256,128]{1,0:T(8,128)S(1)} %bitcast.133, f32[256,128]{1,0:T(8,128)S(1)} %bitcast.135), kind=kOutput, calls=%fused_computation.86 | convolution fusion | flops 406454272 | bytes 786432 | tf_op jit(solution)/shard_map/qp,...pk->...qk/dot_general | solution.py:39
  175.6 1.7 fusion.128
  177.3 14.9 %fusion.127 = f32[128,512]{1,0:T(8,128)} fusion(f32[512,128]{1,0:T(8,128)S(1)} %convolution_add_fusion.3, f32[512,128]{1,0:T(8,128)S(1)} %convolution_subtract_fusion.3), kind=kOutput, calls=%fused_computation.182 | convolution fusion | flops 102006784 | bytes 786432 | tf_op jit(solution)/shard_map/dot_general | solution.py:49
  192.2 1.7 convolution_add_fusion.2
  193.9 0.1 reshape.347
  194.0 2.7 convolution_subtract_fusion.2
  196.7 0.1 reshape.346
  196.7 1.8 multiply_add_fusion.2
  198.5 1.0 copy.42
  199.5 4.1 all-to-all-start
  203.6 0.3 fusion.153
  203.8 0.1 copy.49
  203.9 12.9 %all_gather.11 = f32[3,65536]{1,0:T(4,128)S(1)} all-gather(f32[3,8192]{1,0:T(4,128)S(1)} %select_divide_fusion), channel_id=1, replica_groups=mesh['tm'=4,'tmpl'=8] {'tmpl'}, dimensions={1}, use_global_device_ids=true | all-gather | bytes 884736 | tf_op jit(solution)/shard_map/all_gather | solution.py:139
  216.8 1.5 mul.799
  218.3 1.9 copy.43
  220.2 3.4 all-to-all-start.1
  223.6 0.0 copy-start.5
  223.6 0.0 copy-start.6
  223.6 1.5 fusion.92
  225.1 5.4 %all-to-all-done.1 = f32[8,1,8192]{2,1,0:T(1,128)S(1)} async-done(((f32[8,1,8192]{2,1,0:T(1,128)}), f32[8,1,8192]{2,1,0:T(1,128)S(1)}, u32[]{:S(2)}, u32[]{:S(2)}) %all-to-all-start.1) | async-done | bytes 262176 | tf_op jit(solution)/shard_map/all_to_all | solution.py:130
  230.5 0.7 copy-done.3
  231.2 0.5 fusion.3
  231.7 10.0 %all_gather.10 = f32[3,65536]{1,0:T(4,128)S(1)} all-gather(f32[3,8192]{1,0:T(4,128)S(1)} %fusion.3), channel_id=1, replica_groups=mesh['tm'=4,'tmpl'=8] {'tmpl'}, dimensions={1}, use_global_device_ids=true | all-gather | bytes 884736 | tf_op jit(solution)/shard_map/all_gather | solution.py:138
  241.7 1.5 mul.763
  243.1 1.4 fusion.94
  244.6 1.5 fusion.5
  246.1 11.2 %all_gather.9 = f32[3,65536]{1,0:T(4,128)S(1)} all-gather(f32[3,8192]{1,0:T(4,128)S(1)} %fusion.5), channel_id=1, replica_groups=mesh['tm'=4,'tmpl'=8] {'tmpl'}, dimensions={1}, use_global_device_ids=true | all-gather | bytes 884736 | tf_op jit(solution)/shard_map/all_gather | solution.py:137
  257.3 1.5 mul.743
  258.7 30.0 %multiply_subtract_fusion.1 = (f32[2,196608]{1,0:T(2,128)S(1)}, f32[2,196608]{1,0:T(2,128)S(1)}, f32[2]{0:T(128)S(1)}) fusion(f32[196608]{0:T(1024)} %mul.763, f32[196608]{0:T(1024)} %mul.743, s32[196608]{0:T(1024)} %add_select_fusion.2, s32[2]{0:T(128)S(1)} %copy-done.5, s32[2]{0:T(128)S(1)} %copy-done.6, f32[196608]{0:T(1024)} %get-tuple-element.12, ...), kind=kLoop, calls=%fused_computation.57 | loop fusion | flops 11403262 | bytes 7864344 | tf_op jit(solution)/shard_map/sub | solution.py:149
  288.7 6.9 %pad.7 = f32[2,524288]{1,0:T(2,128)S(1)} pad(f32[2,196608]{1,0:T(2,128)S(1)} %get-tuple-element.8, f32[]{:T(128)} %constant.193.clone.1), padding=0_0x0_327680 | pad | bytes 5767172 | tf_op jit(solution)/shard_map/jit(_pad)/pad | solution.py:151
  295.7 6.6 %fusion.16 = f32[2,16384,32]{1,2,0:T(8,128)S(1)} fusion(f32[1,2,32,16384]{3,1,2,0:T(2,128)S(1)} %bitcast.125), kind=kOutput, calls=%fused_computation.21 | convolution fusion | flops 402667520 | bytes 8388608 | tf_op jit(solution)/shard_map/qp,...pk->...qk/dot_general | solution.py:39
  302.3 6.8 %fusion.18 = f32[2,16384,32]{1,2,0:T(8,128)S(1)} fusion(f32[1,2,32,16384]{3,1,2,0:T(2,128)S(1)} %bitcast.126), kind=kOutput, calls=%fused_computation.23 | convolution fusion | flops 402667520 | bytes 8388608 | tf_op jit(solution)/shard_map/qp,...pk->...qk/dot_general | solution.py:36
  309.1 6.5 %pad.8 = f32[2,524288]{1,0:T(2,128)S(1)} pad(f32[2,196608]{1,0:T(2,128)S(1)} %get-tuple-element.7, f32[]{:T(128)} %constant.193.clone.1), padding=0_0x0_327680 | pad | bytes 5767172 | tf_op jit(solution)/shard_map/jit(_pad)/pad | solution.py:151
  315.6 0.0 copy-start.2
  315.6 6.7 %fusion = f32[2,32,16384]{2,1,0:T(8,128)S(1)} fusion(f32[2,16384,32]{1,2,0:T(8,128)S(1)} %fusion.18, f32[1,2,32,16384]{3,1,2,0:T(2,128)S(1)} %bitcast.121), kind=kOutput, calls=%fused_computation.3 | convolution fusion | flops 403716096 | bytes 12582912 | tf_op jit(solution)/shard_map/qp,...pk->...qk/dot_general | solution.py:36
  322.3 8.5 %multiply_subtract_fusion = (f32[2,32,16384]{2,1,0:T(8,128)}, f32[2,32,16384]{2,1,0:T(8,128)S(1)}) fusion(f32[2,32,16384]{2,1,0:T(8,128)S(1)} %fusion, f32[32,16384]{1,0:T(8,128)S(1)} %get-tuple-element.14, f32[32,16384]{1,0:T(8,128)S(1)} %copy-done.2, f32[2,16384,32]{1,2,0:T(8,128)S(1)} %fusion.16, f32[1,2,32,16384]{3,1,2,0:T(2,128)S(1)} %bitcast.122), kind=kOutput, calls=%fused_computation.33 | convolution fusion | flops 410007552 | bytes 25165824 | tf_op jit(solution)/shard_map/qp,...pk->...qk/dot_general | solution.py:39
  330.8 2.9 copy.69
  333.8 0.7 copy.70
  334.5 7.7 %fusion.8 = f32[2,32,128,128]{3,2,1,0:T(8,128)S(1)} fusion(f32[2,32,128,128]{3,2,1,0:T(8,128)S(1)} %bitcast.127), kind=kOutput, calls=%fused_computation.13 | convolution fusion | flops 1610842112 | bytes 8388608 | tf_op jit(solution)/shard_map/qp,...pk->...qk/dot_general | solution.py:36
  342.2 8.0 %fusion.6 = f32[2,32,128,128]{3,2,1,0:T(8,128)S(1)} fusion(f32[2,32,128,128]{3,2,1,0:T(8,128)S(1)} %bitcast.128), kind=kOutput, calls=%fused_computation.11 | convolution fusion | flops 1610842112 | bytes 8388608 | tf_op jit(solution)/shard_map/qp,...pk->...qk/dot_general | solution.py:39
  350.3 7.8 %fusion.26 = f32[2,32,128,128]{3,2,1,0:T(8,128)S(1)} fusion(f32[2,32,128,128]{3,2,1,0:T(8,128)S(1)} %fusion.8, f32[2,32,128,128]{3,2,1,0:T(8,128)S(1)} %bitcast.123), kind=kOutput, calls=%fused_computation.44 | convolution fusion | flops 1611890688 | bytes 12582912 | tf_op jit(solution)/shard_map/qp,...pk->...qk/dot_general | solution.py:36
  358.0 8.0 %fusion.29 = f32[2,32,128,128]{3,2,1,0:T(8,128)S(1)} fusion(f32[2,32,128,128]{3,2,1,0:T(8,128)S(1)} %fusion.6, f32[2,32,128,128]{3,2,1,0:T(8,128)S(1)} %bitcast.124), kind=kOutput, calls=%fused_computation.45 | convolution fusion | flops 1611890688 | bytes 12582912 | tf_op jit(solution)/shard_map/qp,...pk->...qk/dot_general | solution.py:39
  366.0 7.2 %fusion.48 = f32[2,32,128,128]{3,2,1,0:T(8,128)S(1)} fusion(f32[2,32,128,128]{3,2,1,0:T(8,128)S(1)} %fusion.29, f32[2,32,128,128]{3,2,1,0:T(8,128)S(1)} %fusion.26, f32[128,128]{0,1:T(8,128)S(1)} %copy.49, f32[128,128]{0,1:T(8,128)S(1)} %copy.46), kind=kOutput, calls=%fused_computation.75 | convolution fusion | flops 1613987840 | bytes 12713984 | tf_op jit(solution)/shard_map/dot_general | solution.py:52
  373.2 7.4 %fusion.46 = f32[2,32,128,128]{3,2,1,0:T(8,128)S(1)} fusion(f32[2,32,128,128]{3,2,1,0:T(8,128)S(1)} %fusion.29, f32[2,32,128,128]{3,2,1,0:T(8,128)S(1)} %fusion.26, f32[128,128]{0,1:T(8,128)S(1)} %copy.49, f32[128,128]{0,1:T(8,128)S(1)} %copy.46), kind=kOutput, calls=%fused_computation.74 | convolution fusion | flops 1613987840 | bytes 12713984 | tf_op jit(solution)/shard_map/dot_general | solution.py:49
  380.7 7.1 %fusion.50 = f32[2,32,128,128]{3,2,1,0:T(8,128)S(1)} fusion(f32[2,32,128,128]{3,2,1,0:T(8,128)S(1)} %fusion.29, f32[2,32,128,128]{3,2,1,0:T(8,128)S(1)} %fusion.26, f32[128,128]{0,1:T(8,128)S(1)} %copy.49, f32[128,128]{0,1:T(8,128)S(1)} %copy.46), kind=kOutput, calls=%fused_computation.76 | convolution fusion | flops 1613987840 | bytes 12713984 | tf_op jit(solution)/shard_map/dot_general | solution.py:49
  387.8 9.8 %sqrt_bitcast_fusion = f32[2,128,128,32]{1,2,3,0:T(8,128)} fusion(f32[2,32,128,128]{3,2,1,0:T(8,128)S(1)} %fusion.48, f32[2,32,128,128]{3,2,1,0:T(8,128)S(1)} %fusion.50, f32[2,32,128,128]{3,2,1,0:T(8,128)S(1)} %fusion.46, f32[2,32,128,128]{3,2,1,0:T(8,128)S(1)} %fusion.29, f32[2,32,128,128]{3,2,1,0:T(8,128)S(1)} %fusion.26, f32[128,128]{0,1:T(8,128)S(1)} %copy.49, ...), kind=kOutput, calls=%fused_computation.31 | convolution fusion | flops 1619230720 | bytes 25296896 | tf_op jit(solution)/shard_map/dot_general | solution.py:52
  397.6 14.8 %copy.54 = f32[2,128,128,32]{3,2,1,0:T(8,128)} copy(f32[2,128,128,32]{1,2,3,0:T(8,128)} %sqrt_bitcast_fusion) | data formatting | bytes 8388608 | tf_op jit(solution)/shard_map/sqrt | solution.py:153
  412.4 0.0 copy-start.1
  412.4 15.7 %sqrt.18 = f32[2,524288]{1,0:T(2,128)} reshape(f32[2,128,128,32]{3,2,1,0:T(8,128)} %copy.54) | data formatting | bytes 8388608 | tf_op jit(solution)/shard_map/sqrt | solution.py:153
  428.1 3.1 slice_divide_fusion
  (17 shorter events, 0.1 us)
Async XLA Ops:
  0.0 23.5 %copy-start = (f32[1,8192]{1,0:T(1,128)S(1)}, f32[1,8192]{1,0:T(1,128)}, u32[]{:S(2)}) copy-start(f32[1,8192]{1,0:T(1,128)} %param.7) | copy-start | bytes 98308
  0.0 165.1 %collective-permute-start = (f32[32768]{0:T(1024)}, f32[32768]{0:T(1024)S(1)}, u32[]{:S(2)}, u32[]{:S(2)}) collective-permute-start(f32[32768]{0:T(1024)} %bitcast.131), channel_id=1, source_target_pairs={{0,8},{8,16},{16,24},{1,9},{9,17},{17,25},{2,10},{10,18},{18,26},{... | collective-permute-start | bytes 393224 | tf_op jit(solution)/shard_map/ppermute | solution.py:15
  11.0 12.4 %copy-start.4 = (s32[4,8192]{1,0:T(4,128)S(1)}, s32[4,8192]{1,0:T(4,128)}, u32[]{:S(2)}) copy-start(s32[4,8192]{1,0:T(4,128)} %param.6) | copy-start | bytes 393220
  159.1 6.0 %copy-start.7 = (f32[1,32768]{1,0:T(1,128)S(1)}, f32[1,32768]{1,0:T(1,128)}, u32[]{:S(2)}) copy-start(f32[1,32768]{1,0:T(1,128)} %param.5) | copy-start | bytes 393220
  175.6 16.6 %copy-start.8 = (f32[512,128]{1,0:T(8,128)}, f32[512,128]{1,0:T(8,128)S(1)}, u32[]{:S(2)}) copy-start(f32[512,128]{1,0:T(8,128)S(1)} %convolution_add_fusion.3) | copy-start | bytes 786436
  199.5 20.7 %all-to-all-start = ((f32[8,1,8192]{2,1,0:T(1,128)}), f32[8,1,8192]{2,1,0:T(1,128)}, u32[]{:S(2)}, u32[]{:S(2)}) async-start(f32[8,1,8192]{2,1,0:T(1,128)} %copy.42), calls=%async_computation | async-start | bytes 524288 | tf_op jit(solution)/shard_map/all_to_all | solution.py:127
  220.2 10.3 %all-to-all-start.1 = ((f32[8,1,8192]{2,1,0:T(1,128)}), f32[8,1,8192]{2,1,0:T(1,128)S(1)}, u32[]{:S(2)}, u32[]{:S(2)}) async-start(f32[8,1,8192]{2,1,0:T(1,128)} %copy.43), calls=%async_computation.1 | async-start | bytes 524288 | tf_op jit(solution)/shard_map/all_to_all | solution.py:130
  223.6 35.1 %copy-start.5 = (s32[2]{0:T(128)S(1)}, s32[2]{0:T(128)}, u32[]{:S(2)}) copy-start(s32[2]{0:T(128)} %param.9) | copy-start | bytes 28
  223.6 35.1 %copy-start.6 = (s32[2]{0:T(128)S(1)}, s32[2]{0:T(128)}, u32[]{:S(2)}) copy-start(s32[2]{0:T(128)} %param.8) | copy-start | bytes 28
  230.5 0.7 copy-start.3
  315.6 6.7 %copy-start.2 = (f32[32,16384]{1,0:T(8,128)S(1)}, f32[32,16384]{1,0:T(8,128)}, u32[]{:S(2)}) copy-start(f32[32,16384]{1,0:T(8,128)} %get-tuple-element.15) | copy-start | bytes 6291460
  412.4 18.8 %copy-start.1 = (f32[1,8192]{1,0:T(1,128)S(1)}, f32[1,8192]{1,0:T(1,128)}, u32[]{:S(2)}) copy-start(f32[1,8192]{1,0:T(1,128)} %param.7) | copy-start | bytes 98308
where the time goes:
time: 437 us; the launch traced here: 432 us
  local copies, waits for them, and re-layouts  192 us (44%)
  matrix products  139 us (32%)
  other arithmetic  47.9 us (11%)
  blocking collectives  34.1 us (8%)
  starting transfers between devices  12.6 us (3%)
  waiting for transfers between devices  5.36 us (1%)
    gather x2, local copies, waits for them, and re-layouts, local(): inv_psd = 1.0 / jnp.take(psd_values[0], psd_bins[:band_rows])  136 us
    sqrt x2, local copies, waits for them, and re-layouts, local(): jnp.sqrt(series_re * series_re + series_im * series_im)  30.5 us
    sub x1, other arithmetic, local(): coef_im = white_im * tmpl_re - white_re * tmpl_im  30 us
    dot_general x4, matrix products, complex_left(): jnp.einsum('qp,...pk->...qk', cos_part, imag_part, precision=HIGHEST)  22.6 us
    dot_general x2, matrix products, apply_sizes(): jnp.matmul(real_part, cos_part, precision=HIGHEST)  22 us
    dot_general x4, matrix products, complex_left(): jnp.einsum('qp,...pk->...qk', cos_part, real_part, precision=HIGHEST)  21.7 us
    dot_general x4, matrix products, complex_left(): jnp.einsum('qp,...pk->...qk', sin_part, imag_part, precision=HIGHEST)  21.7 us
    dot_general x4, matrix products, complex_left(): jnp.einsum('qp,...pk->...qk', sin_part, real_part, precision=HIGHEST)  20.8 us
  transfers between devices with their start and end apart: 3, of which 1 were waited for; matrix products, arithmetic and copies ran while one was open for 38% of the time, Pallas kernels for 0%

commit v1 on v0

--- a/solution.py
+++ b/solution.py
@@ -7,6 +7,12 @@
 OR = 32768
 HIGHEST = lax.Precision.HIGHEST
 TWO_PI = 2.0 * math.pi
+_balance_modes = lambda vector, net_axis: jnp.concatenate(
+    lax.all_to_all(
+        jnp.stack(jnp.split(vector, lax.axis_size(net_axis), axis=0), axis=0), net_axis, 0, 0
+    ),
+    axis=1,
+)
 
 
 def shifted(block, axis, distance):
@@ -127,9 +133,7 @@
     piece_re = lax.all_to_all(
         part_re.reshape(groups, 1, block_len), "tmpl", split_axis=0, concat_axis=1, tiled=True
     )
-    piece_im = lax.all_to_all(
-        part_im.reshape(groups, 1, block_len), "tmpl", split_axis=0, concat_axis=1, tiled=True
-    )
+    piece_im = _balance_modes(part_im.reshape(groups, 1, block_len), "tmpl")
     spec_re, spec_im = complex_left(cross_cos, cross_sin, piece_re[0], piece_im[0])
     white_re = spec_re * inv_psd * norm_scale
     white_im = spec_im * inv_psd * norm_scale

time: 437 us -> 444 us (1.016)
    unnamed x20 -> x33, local copies, waits for them, and re-layouts: 4.42 us -> 8.86 us
  transfers between devices with their start and end apart: 3 -> 3, of which waited for: 1 -> 2; matrix products, arithmetic and copies ran while one was open for 38% -> 38% of each run, Pallas kernels for 0% -> 0%
where the time goes in v1:
time: 444 us; the launch traced here: 437 us
  local copies, waits for them, and re-layouts  196 us (44%)
  matrix products  139 us (31%)
  other arithmetic  48.9 us (11%)
  blocking collectives  32.1 us (7%)
  starting transfers between devices  12.6 us (3%)
  waiting for transfers between devices  8.87 us (2%)
    gather x2, local copies, waits for them, and re-layouts, local(): inv_psd = 1.0 / jnp.take(psd_values[0], psd_bins[:band_rows])  136 us
    sqrt x2, local copies, waits for them, and re-layouts, local(): jnp.sqrt(series_re * series_re + series_im * series_im)  30.4 us
    sub x1, other arithmetic, local(): coef_im = white_im * tmpl_re - white_re * tmpl_im  30 us
    dot_general x4, matrix products, complex_left(): jnp.einsum('qp,...pk->...qk', cos_part, imag_part, precision=HIGHEST)  22.5 us
    dot_general x4, matrix products, complex_left(): jnp.einsum('qp,...pk->...qk', cos_part, real_part, precision=HIGHEST)  21.7 us
    dot_general x4, matrix products, complex_left(): jnp.einsum('qp,...pk->...qk', sin_part, imag_part, precision=HIGHEST)  21.7 us
    dot_general x2, matrix products, apply_sizes(): jnp.matmul(real_part, cos_part, precision=HIGHEST)  21.3 us
    dot_general x4, matrix products, complex_left(): jnp.einsum('qp,...pk->...qk', sin_part, real_part, precision=HIGHEST)  20.8 us
  transfers between devices with their start and end apart: 3, of which 2 were waited for; matrix products, arithmetic and copies ran while one was open for 38% of the time, Pallas kernels for 0%

profile of v1, /device:TPU:0, one launch (start us, length us, event | category | flops | bytes accessed | tf_op | source)
XLA Modules:
  0.0 437.4 jit_solution(14373833632578255004)
XLA Ops:
  0.0 5.7 %collective-permute-start = (f32[32768]{0:T(1024)}, f32[32768]{0:T(1024)}, u32[]{:S(2)}, u32[]{:S(2)}) collective-permute-start(f32[32768]{0:T(1024)} %bitcast.155), channel_id=1, source_target_pairs={{0,8},{8,16},{16,24},{1,9},{9,17},{17,25},{2,10},{10,18},{18,26},{... | collective-permute-start | bytes 393224 | tf_op jit(solution)/shard_map/ppermute | solution.py:21
  5.7 0.3 fusion.158
  6.0 5.9 %fusion.81 = f32[512,128]{1,0:T(8,128)} fusion(), kind=kOutput, calls=%fused_computation.114 | convolution fusion | flops 406323200 | bytes 262144 | tf_op jit(solution)/shard_map/qp,...pk->...qk/dot_general | solution.py:42
  11.9 1.7 add_select_fusion.2
  13.5 1.7 fusion.71
  15.2 9.1 %fusion.55 = (f32[32,16384]{1,0:T(8,128)S(1)}, f32[32,16384]{1,0:T(8,128)}) fusion(), kind=kLoop, calls=%fused_computation.91 | loop fusion | flops 7340032 | bytes 4194304 | tf_op jit(solution)/shard_map/sin | solution.py:38
  24.4 135.5 %gather_fusion = f32[24576]{0:T(1024)S(1)} fusion(f32[8192]{0:T(1024)S(1)} %bitcast.132, s32[24576]{0:T(1024)S(1)} %broadcast_clamp_fusion), kind=kCustom, calls=%fused_computation | custom fusion | bytes 294912 | tf_op jit(solution)/shard_map/jit(_take)/gather | solution.py:124
  160.0 0.1 select_divide_fusion
  160.1 11.0 %all_gather.11 = f32[3,65536]{1,0:T(4,128)S(1)} all-gather(f32[3,8192]{1,0:T(4,128)S(1)} %select_divide_fusion), channel_id=1, replica_groups=mesh['tm'=4,'tmpl'=8] {'tmpl'}, dimensions={1}, use_global_device_ids=true | all-gather | bytes 884736 | tf_op jit(solution)/shard_map/all_gather | solution.py:143
  171.1 0.9 fusion.157
  172.0 0.1 copy.43
  172.1 0.9 copy.46
  173.0 1.5 mul.789
  174.5 5.5 %fusion.77 = f32[512,128]{1,0:T(8,128)S(1)} fusion(), kind=kOutput, calls=%fused_computation.113 | convolution fusion | flops 406323200 | bytes 262144 | tf_op jit(solution)/shard_map/qp,...pk->...qk/dot_general | solution.py:45
  180.0 5.7 %convolution_subtract_fusion.3 = f32[512,128]{1,0:T(8,128)S(1)} fusion(f32[512,128]{1,0:T(8,128)S(1)} %copy-done.10, f32[256,128]{1,0:T(8,128)} %bitcast.156, f32[256,128]{1,0:T(8,128)} %bitcast.1), kind=kOutput, calls=%fused_computation.87 | convolution fusion | flops 406454272 | bytes 786432 | tf_op jit(solution)/shard_map/qp,...pk->...qk/dot_general | solution.py:42
  185.7 5.7 %convolution_add_fusion.3 = f32[512,128]{1,0:T(8,128)S(1)} fusion(f32[512,128]{1,0:T(8,128)S(1)} %fusion.77, f32[256,128]{1,0:T(8,128)S(1)} %bitcast.157, f32[256,128]{1,0:T(8,128)} %bitcast.1), kind=kOutput, calls=%fused_computation.86 | convolution fusion | flops 406454272 | bytes 786432 | tf_op jit(solution)/shard_map/qp,...pk->...qk/dot_general | solution.py:45
  191.4 1.7 fusion.132
  193.1 14.2 %fusion.131 = f32[128,512]{1,0:T(8,128)} fusion(f32[512,128]{1,0:T(8,128)S(1)} %convolution_add_fusion.3, f32[512,128]{1,0:T(8,128)S(1)} %convolution_subtract_fusion.3), kind=kOutput, calls=%fused_computation.189 | convolution fusion | flops 102006784 | bytes 786432 | tf_op jit(solution)/shard_map/dot_general | solution.py:55
  207.3 1.7 convolution_add_fusion.2
  209.2 2.7 convolution_subtract_fusion.2
  212.0 1.1 multiply_add_fusion.2
  213.1 0.6 constant_dynamic-update-slice_fusion.7
  213.8 1.1 multiply_subtract_fusion.2
  214.9 1.0 copy.40
  215.9 3.4 all-to-all-start
  219.3 0.6 constant_dynamic-update-slice_fusion.6
  219.9 0.6 constant_dynamic-update-slice_fusion.5
  220.5 0.6 constant_dynamic-update-slice_fusion.4
  221.1 0.6 constant_dynamic-update-slice_fusion.3
  221.7 0.6 constant_dynamic-update-slice_fusion.2
  222.4 0.6 constant_dynamic-update-slice_fusion.1
  223.0 0.6 constant_dynamic-update-slice_fusion
  223.6 2.6 all-to-all-done
  226.1 3.4 all-to-all-start.1
  229.6 0.5 fusion.95
  230.1 6.3 %all-to-all-done.1 = f32[8,1,1,8192]{3,2,1,0:T(1,128)S(1)} async-done(((f32[8,1,1,8192]{3,2,1,0:T(1,128)}), f32[8,1,1,8192]{3,2,1,0:T(1,128)S(1)}, u32[]{:S(2)}, u32[]{:S(2)}) %all-to-all-start.1) | async-done | bytes 262176 | tf_op jit(solution)/shard_map/all_to_all | solution.py:11
  236.4 0.7 copy-done.4
  237.1 0.5 fusion.3
  237.6 10.0 %all_gather.10 = f32[3,65536]{1,0:T(4,128)S(1)} all-gather(f32[3,8192]{1,0:T(4,128)S(1)} %fusion.3), channel_id=1, replica_groups=mesh['tm'=4,'tmpl'=8] {'tmpl'}, dimensions={1}, use_global_device_ids=true | all-gather | bytes 884736 | tf_op jit(solution)/shard_map/all_gather | solution.py:142
  247.6 1.5 mul.753
  249.1 1.4 fusion.97
  250.5 1.5 fusion.5
  252.0 11.2 %all_gather.9 = f32[3,65536]{1,0:T(4,128)S(1)} all-gather(f32[3,8192]{1,0:T(4,128)S(1)} %fusion.5), channel_id=1, replica_groups=mesh['tm'=4,'tmpl'=8] {'tmpl'}, dimensions={1}, use_global_device_ids=true | all-gather | bytes 884736 | tf_op jit(solution)/shard_map/all_gather | solution.py:141
  263.2 1.5 mul.733
  264.7 30.0 %multiply_subtract_fusion.1 = (f32[2,196608]{1,0:T(2,128)S(1)}, f32[2,196608]{1,0:T(2,128)S(1)}, f32[2]{0:T(128)S(1)}) fusion(f32[196608]{0:T(1024)} %mul.753, f32[196608]{0:T(1024)} %mul.733, s32[196608]{0:T(1024)} %add_select_fusion.2, s32[2]{0:T(128)S(1)} %copy-done.6, s32[2]{0:T(128)S(1)} %copy-done.7, f32[196608]{0:T(1024)} %get-tuple-element.18, ...), kind=kLoop, calls=%fused_computation.57 | loop fusion | flops 11403262 | bytes 7864344 | tf_op jit(solution)/shard_map/sub | solution.py:153
  294.7 6.9 %pad.7 = f32[2,524288]{1,0:T(2,128)S(1)} pad(f32[2,196608]{1,0:T(2,128)S(1)} %get-tuple-element.8, f32[]{:T(128)} %constant.192.clone.1), padding=0_0x0_327680 | pad | bytes 5767172 | tf_op jit(solution)/shard_map/jit(_pad)/pad | solution.py:155
  301.6 6.6 %fusion.16 = f32[2,16384,32]{1,2,0:T(8,128)S(1)} fusion(f32[1,2,32,16384]{3,1,2,0:T(2,128)S(1)} %bitcast.137), kind=kOutput, calls=%fused_computation.21 | convolution fusion | flops 402667520 | bytes 8388608 | tf_op jit(solution)/shard_map/qp,...pk->...qk/dot_general | solution.py:45
  308.2 6.8 %fusion.18 = f32[2,16384,32]{1,2,0:T(8,128)S(1)} fusion(f32[1,2,32,16384]{3,1,2,0:T(2,128)S(1)} %bitcast.138), kind=kOutput, calls=%fused_computation.23 | convolution fusion | flops 402667520 | bytes 8388608 | tf_op jit(solution)/shard_map/qp,...pk->...qk/dot_general | solution.py:42
  315.0 6.5 %pad.8 = f32[2,524288]{1,0:T(2,128)S(1)} pad(f32[2,196608]{1,0:T(2,128)S(1)} %get-tuple-element.7, f32[]{:T(128)} %constant.192.clone.1), padding=0_0x0_327680 | pad | bytes 5767172 | tf_op jit(solution)/shard_map/jit(_pad)/pad | solution.py:155
  321.6 6.7 %fusion = f32[2,32,16384]{2,1,0:T(8,128)S(1)} fusion(f32[2,16384,32]{1,2,0:T(8,128)S(1)} %fusion.18, f32[1,2,32,16384]{3,1,2,0:T(2,128)S(1)} %bitcast.133), kind=kOutput, calls=%fused_computation.3 | convolution fusion | flops 403716096 | bytes 12582912 | tf_op jit(solution)/shard_map/qp,...pk->...qk/dot_general | solution.py:42
  328.3 8.5 %multiply_subtract_fusion = (f32[2,32,16384]{2,1,0:T(8,128)}, f32[2,32,16384]{2,1,0:T(8,128)S(1)}) fusion(f32[2,32,16384]{2,1,0:T(8,128)S(1)} %fusion, f32[32,16384]{1,0:T(8,128)S(1)} %get-tuple-element.20, f32[32,16384]{1,0:T(8,128)S(1)} %copy-done.2, f32[2,16384,32]{1,2,0:T(8,128)S(1)} %fusion.16, f32[1,2,32,16384]{3,1,2,0:T(2,128)S(1)} %bitcast.134), kind=kOutput, calls=%fused_computation.33 | convolution fusion | flops 410007552 | bytes 25165824 | tf_op jit(solution)/shard_map/qp,...pk->...qk/dot_general | solution.py:45
  336.8 2.9 copy.68
  339.7 0.7 copy.69
  340.4 7.7 %fusion.8 = f32[2,32,128,128]{3,2,1,0:T(8,128)S(1)} fusion(f32[2,32,128,128]{3,2,1,0:T(8,128)S(1)} %bitcast.139), kind=kOutput, calls=%fused_computation.13 | convolution fusion | flops 1610842112 | bytes 8388608 | tf_op jit(solution)/shard_map/qp,...pk->...qk/dot_general | solution.py:42
  348.1 8.0 %fusion.6 = f32[2,32,128,128]{3,2,1,0:T(8,128)S(1)} fusion(f32[2,32,128,128]{3,2,1,0:T(8,128)S(1)} %bitcast.140), kind=kOutput, calls=%fused_computation.11 | convolution fusion | flops 1610842112 | bytes 8388608 | tf_op jit(solution)/shard_map/qp,...pk->...qk/dot_general | solution.py:45
  356.2 7.8 %fusion.26 = f32[2,32,128,128]{3,2,1,0:T(8,128)S(1)} fusion(f32[2,32,128,128]{3,2,1,0:T(8,128)S(1)} %fusion.8, f32[2,32,128,128]{3,2,1,0:T(8,128)S(1)} %bitcast.135), kind=kOutput, calls=%fused_computation.44 | convolution fusion | flops 1611890688 | bytes 12582912 | tf_op jit(solution)/shard_map/qp,...pk->...qk/dot_general | solution.py:42
  363.9 8.0 %fusion.29 = f32[2,32,128,128]{3,2,1,0:T(8,128)S(1)} fusion(f32[2,32,128,128]{3,2,1,0:T(8,128)S(1)} %fusion.6, f32[2,32,128,128]{3,2,1,0:T(8,128)S(1)} %bitcast.136), kind=kOutput, calls=%fused_computation.45 | convolution fusion | flops 1611890688 | bytes 12582912 | tf_op jit(solution)/shard_map/qp,...pk->...qk/dot_general | solution.py:45
  371.9 7.2 %fusion.48 = f32[2,32,128,128]{3,2,1,0:T(8,128)S(1)} fusion(f32[2,32,128,128]{3,2,1,0:T(8,128)S(1)} %fusion.29, f32[2,32,128,128]{3,2,1,0:T(8,128)S(1)} %fusion.26, f32[128,128]{0,1:T(8,128)S(1)} %copy.46, f32[128,128]{0,1:T(8,128)S(1)} %copy.43), kind=kOutput, calls=%fused_computation.75 | convolution fusion | flops 1613987840 | bytes 12713984 | tf_op jit(solution)/shard_map/dot_general | solution.py:58
  379.2 7.4 %fusion.46 = f32[2,32,128,128]{3,2,1,0:T(8,128)S(1)} fusion(f32[2,32,128,128]{3,2,1,0:T(8,128)S(1)} %fusion.29, f32[2,32,128,128]{3,2,1,0:T(8,128)S(1)} %fusion.26, f32[128,128]{0,1:T(8,128)S(1)} %copy.46, f32[128,128]{0,1:T(8,128)S(1)} %copy.43), kind=kOutput, calls=%fused_computation.74 | convolution fusion | flops 1613987840 | bytes 12713984 | tf_op jit(solution)/shard_map/dot_general | solution.py:55
  386.6 7.1 %fusion.50 = f32[2,32,128,128]{3,2,1,0:T(8,128)S(1)} fusion(f32[2,32,128,128]{3,2,1,0:T(8,128)S(1)} %fusion.29, f32[2,32,128,128]{3,2,1,0:T(8,128)S(1)} %fusion.26, f32[128,128]{0,1:T(8,128)S(1)} %copy.46, f32[128,128]{0,1:T(8,128)S(1)} %copy.43), kind=kOutput, calls=%fused_computation.76 | convolution fusion | flops 1613987840 | bytes 12713984 | tf_op jit(solution)/shard_map/dot_general | solution.py:55
  393.7 9.8 %sqrt_bitcast_fusion = f32[2,128,128,32]{1,2,3,0:T(8,128)} fusion(f32[2,32,128,128]{3,2,1,0:T(8,128)S(1)} %fusion.48, f32[2,32,128,128]{3,2,1,0:T(8,128)S(1)} %fusion.50, f32[2,32,128,128]{3,2,1,0:T(8,128)S(1)} %fusion.46, f32[2,32,128,128]{3,2,1,0:T(8,128)S(1)} %fusion.29, f32[2,32,128,128]{3,2,1,0:T(8,128)S(1)} %fusion.26, f32[128,128]{0,1:T(8,128)S(1)} %copy.46, ...), kind=kOutput, calls=%fused_computation.31 | convolution fusion | flops 1619230720 | bytes 25296896 | tf_op jit(solution)/shard_map/dot_general | solution.py:58
  403.5 14.7 %copy.51 = f32[2,128,128,32]{3,2,1,0:T(8,128)} copy(f32[2,128,128,32]{1,2,3,0:T(8,128)} %sqrt_bitcast_fusion) | data formatting | bytes 8388608 | tf_op jit(solution)/shard_map/sqrt | solution.py:157
  418.2 15.7 %sqrt.18 = f32[2,524288]{1,0:T(2,128)} reshape(f32[2,128,128,32]{3,2,1,0:T(8,128)} %copy.51) | data formatting | bytes 8388608 | tf_op jit(solution)/shard_map/sqrt | solution.py:157
  433.9 3.1 slice_divide_fusion
  (32 shorter events, 0.5 us)
Async XLA Ops:
  0.0 24.4 %copy-start = (f32[1,8192]{1,0:T(1,128)S(1)}, f32[1,8192]{1,0:T(1,128)}, u32[]{:S(2)}) copy-start(f32[1,8192]{1,0:T(1,128)} %param.7) | copy-start | bytes 98308
  0.0 180.0 %collective-permute-start = (f32[32768]{0:T(1024)}, f32[32768]{0:T(1024)}, u32[]{:S(2)}, u32[]{:S(2)}) collective-permute-start(f32[32768]{0:T(1024)} %bitcast.155), channel_id=1, source_target_pairs={{0,8},{8,16},{16,24},{1,9},{9,17},{17,25},{2,10},{10,18},{18,26},{... | collective-permute-start | bytes 393224 | tf_op jit(solution)/shard_map/ppermute | solution.py:21
  11.9 12.4 %copy-start.5 = (s32[4,8192]{1,0:T(4,128)S(1)}, s32[4,8192]{1,0:T(4,128)}, u32[]{:S(2)}) copy-start(s32[4,8192]{1,0:T(4,128)} %param.6) | copy-start | bytes 393220
  174.5 5.5 %copy-start.10 = (f32[512,128]{1,0:T(8,128)S(1)}, f32[512,128]{1,0:T(8,128)}, u32[]{:S(2)}) copy-start(f32[512,128]{1,0:T(8,128)} %fusion.81) | copy-start | bytes 786436
  174.5 11.2 %copy-start.8 = (f32[1,32768]{1,0:T(1,128)S(1)}, f32[1,32768]{1,0:T(1,128)}, u32[]{:S(2)}) copy-start(f32[1,32768]{1,0:T(1,128)} %param.5) | copy-start | bytes 393220
  191.4 15.9 %copy-start.9 = (f32[512,128]{1,0:T(8,128)}, f32[512,128]{1,0:T(8,128)S(1)}, u32[]{:S(2)}) copy-start(f32[512,128]{1,0:T(8,128)S(1)} %convolution_add_fusion.3) | copy-start | bytes 786436
  215.9 10.3 %all-to-all-start = ((f32[8,1,8192]{2,1,0:T(1,128)}), f32[8,1,8192]{2,1,0:T(1,128)S(1)}, u32[]{:S(2)}, u32[]{:S(2)}) async-start(f32[8,1,8192]{2,1,0:T(1,128)} %copy.40), calls=%async_computation | async-start | bytes 524288 | tf_op jit(solution)/shard_map/all_to_all | solution.py:133
  226.1 10.3 %copy-start.3 = (f32[8,1,8192]{2,1,0:T(1,128)}, f32[8,1,8192]{2,1,0:T(1,128)S(1)}, u32[]{:S(2)}) copy-start(f32[8,1,8192]{2,1,0:T(1,128)S(1)} %all-to-all-done) | copy-start | bytes 786436
  226.1 10.3 %all-to-all-start.1 = ((f32[8,1,1,8192]{3,2,1,0:T(1,128)}), f32[8,1,1,8192]{3,2,1,0:T(1,128)S(1)}, u32[]{:S(2)}, u32[]{:S(2)}) async-start(f32[8,1,1,8192]{3,2,1,0:T(1,128)} %constant_dynamic-update-slice_fusion), calls=%async_computation.1 | async-start | bytes 524288 | tf_op jit(solution)/shard_map/all_to_all | solution.py:11
  229.6 35.1 %copy-start.6 = (s32[2]{0:T(128)S(1)}, s32[2]{0:T(128)}, u32[]{:S(2)}) copy-start(s32[2]{0:T(128)} %param.9) | copy-start | bytes 28
  229.6 35.1 %copy-start.7 = (s32[2]{0:T(128)S(1)}, s32[2]{0:T(128)}, u32[]{:S(2)}) copy-start(s32[2]{0:T(128)} %param.8) | copy-start | bytes 28
  236.4 0.7 copy-start.4
  321.6 6.7 %copy-start.2 = (f32[32,16384]{1,0:T(8,128)S(1)}, f32[32,16384]{1,0:T(8,128)}, u32[]{:S(2)}) copy-start(f32[32,16384]{1,0:T(8,128)} %get-tuple-element.21) | copy-start | bytes 6291460
  418.2 18.8 %copy-start.1 = (f32[1,8192]{1,0:T(1,128)S(1)}, f32[1,8192]{1,0:T(1,128)}, u32[]{:S(2)}) copy-start(f32[1,8192]{1,0:T(1,128)} %param.7) | copy-start | bytes 98308
